TPU v7x, 32 devices: a whole 2x2x4 slice. The times are simulated.
32 devices in a mesh: groups: 2 (over y), visits: 16 (over z, x, core).
Axes of the slice: x: 2, y: 2, z: 4, core: 2. Of those that a mesh axis runs over, the one named last changes fastest.
Arguments:
- exposure: float32 [224, 8, 128], P(('groups', 'visits')), parts along dimension 0, may hold values from -6 to 6
- patch_of: int32 [224], P(('groups', 'visits')), parts along dimension 0, may hold values from -1 to 15, as said below
- affine: int32 [6, 224], P(None, ('groups', 'visits')), parts along dimension 1, may hold values from -2048 to 2048, as said below
- psf_weights: float32 [2, 4, 224], P(None, None, ('groups', 'visits')), parts along dimension 2, may hold values from 0.25 to 1
- psf_basis: float32 [2, 4, 21], replicated, may hold values from -2 to 2
- detect_taps: float32 [2, 21], replicated, may hold values from -2 to 2
Outputs:
- template: bfloat16 [32, 8, 128], P(('groups', 'visits')), parts along dimension 0
- difference: float32 [224, 8, 128], P(('groups', 'visits')), parts along dimension 0
- detection: float32 [224, 8, 128], P(('groups', 'visits')), parts along dimension 0
There are 2 independent parts, one for each index of `groups`. A program takes and returns all parts, laid end to end along the dimension named above; an argument that names none is the same for every part. Nothing has to cross between parts.
Inputs may be any that keep to these rules, and one draw needn't show every extreme that they name: `patch_of`: within the slots of one visit no patch appears twice. Every patch is intersected by between 3 and 16 tile slots, and in every draw some patch by exactly 16 and some by exactly 3. `affine`: rows 0 and 4 lie in 240 to 272, rows 1 and 3 in -16 to 16, row 2 in -128 to 128, row 5 in -2048 to 2048.
All inputs are finite; a program needn't handle non-finite values.
Results may differ from a plain program's by a relative error of at most 0.0039.
Values may be sent and summed in bfloat16 or wider, within the bound.
No kernel may reach another device: no remote copies, remote signals or barrier semaphores. Data moves between devices by JAX's collectives and lax.ppermute only.
A program may use at most 64 MiB of HBM per device.

v0:
```python
import jax
import jax.numpy as jnp
from jax import lax
from jax.experimental import pallas as pl
from jax.experimental.pallas import tpu as pltpu
from jax.sharding import PartitionSpec as P


CHUNK = 7
UNROLL_LIMIT = 2048
ON_CHIP_LIMIT = 1 << 19


def round_up(value, step):
    return -(-value // step) * step


def block_rows(tiles, height):
    return round_up(tiles * height + round_up(tiles, height), 2 * height)


def reaches(taps, extent):
    centre = (taps - 1) // 2
    return [(p, p - centre) for p in range(taps) if abs(p - centre) < extent]


def col_tap_vector(value, reach, shape):
    cols = lax.broadcasted_iota(jnp.int32, shape, 1)
    inside = cols < shape[1] - reach if reach > 0 else cols >= -reach
    return jnp.where(inside, value, 0.0)


def row_tap_vector(value, reach, shape):
    rows = lax.broadcasted_iota(jnp.int32, shape, 0)
    inside = rows >= reach if reach > 0 else rows < shape[0] + reach
    return jnp.where(inside, value, 0.0)


def tap_filter(strips, rank, taps, row_tap, col_tap, weight):
    height, extent = strips[0].shape
    partial = [[None] * rank for _ in strips]
    for q, reach in reaches(taps, extent):
        scale = [col_tap(k, q, reach) for k in range(rank)]
        for e, strip in enumerate(strips):
            moved = pltpu.roll(strip, (-reach) % extent, 1) if reach else strip
            for k in range(rank):
                term = scale[k] * moved
                partial[e][k] = term if partial[e][k] is None else partial[e][k] + term
    if weight is not None:
        partial = [[weight(k, e) * partial[e][k] for k in range(rank)] for e in range(len(strips))]
    totals = [None] * len(strips)
    for p, reach in reaches(taps, height):
        scale = [row_tap(k, p, reach) for k in range(rank)]
        for e in range(len(strips)):
            mixed = scale[0] * partial[e][0]
            for k in range(1, rank):
                mixed = mixed + scale[k] * partial[e][k]
            if reach:
                mixed = pltpu.roll(mixed, (-reach) % height, 0)
            totals[e] = mixed if totals[e] is None else totals[e] + mixed
    return totals


def warp_strip(strip, coeff):
    height, extent = strip.shape
    rows = lax.broadcasted_iota(jnp.int32, (height, extent), 0)
    cols = lax.broadcasted_iota(jnp.int32, (height, extent), 1)
    src_row = jnp.clip((coeff(0) * rows + coeff(1) * cols + coeff(2)) >> 8, 0, height - 1)
    src_col = jnp.clip((coeff(3) * rows + coeff(4) * cols + coeff(5)) >> 8, 0, extent - 1)
    warped = jnp.zeros_like(strip)
    for r in range(height):
        line = jnp.broadcast_to(strip[r : r + 1, :], (height, extent))
        picked = jnp.take_along_axis(line, src_col, axis=1, mode="promise_in_bounds")
        warped = jnp.where(src_row == r, picked, warped)
    return warped


def match_kernel(exposure, patch_of, affine, psf_weights, psf_basis, warped_out, block_out):
    tiles, height, extent = exposure.shape
    rank, taps = psf_basis.shape[1:]
    pieces = []
    for first in range(0, tiles, CHUNK):
        chunk = range(first, min(first + CHUNK, tiles))
        strips = []
        for e in chunk:
            strips.append(warp_strip(exposure[e], lambda row, e=e: affine[row, e]))
            warped_out[e] = strips[-1]
        pieces += tap_filter(
            strips,
            rank,
            taps,
            lambda k, p, reach: row_tap_vector(psf_basis[0, k, p], reach, (height, extent)),
            lambda k, q, reach: col_tap_vector(psf_basis[1, k, q], reach, (height, extent)),
            lambda k, i, first=first: psf_weights[0, k, first + i],
        )
    rows = lax.broadcasted_iota(jnp.int32, (height, extent), 0)
    for first in range(0, tiles, height):
        ids = jnp.full((height, extent), -1, jnp.int32)
        for t in range(first, min(first + height, tiles)):
            ids = jnp.where(rows == t - first, patch_of[t], ids)
        pieces.append(ids.astype(jnp.float32))
    while len(pieces) * height < block_out.shape[0]:
        pieces.append(jnp.full((height, extent), -1.0, jnp.float32))
    for i in range(0, len(pieces), 2):
        pair = jnp.concatenate(pieces[i : i + 2], axis=0)
        block_out[i * height : (i + 2) * height, :] = pair.astype(jnp.bfloat16)


def sorting_pairs(count):
    pairs = []
    p = 1
    while p < count:
        k = p
        while k >= 1:
            for j in range(k % p, count - k, 2 * k):
                for i in range(min(k, count - j - k)):
                    if (i + j) // (2 * p) == (i + j + k) // (2 * p):
                        pairs.append((i + j, i + j + k))
            k //= 2
        p *= 2
    return pairs


def fill_missing(candidates, fill):
    far = jnp.full(candidates[0].shape, jnp.inf, jnp.float32)
    values = []
    for value in candidates:
        missing = value == far
        values.append(jnp.where(missing, fill, value))
        fill = jnp.where(missing, -fill, fill)
    return values, fill


def sort_values(values):
    values = list(values)
    for low, high in sorting_pairs(len(values)):
        a, b = values[low], values[high]
        values[low], values[high] = jnp.minimum(a, b), jnp.maximum(a, b)
    return values


def middle(lower, upper, fill):
    upper = jnp.where(fill > 0, upper, lower)
    return ((lower + upper) * 0.5).astype(jnp.bfloat16).astype(jnp.float32)


def median_of(candidates):
    values, fill = fill_missing(candidates, jnp.full(candidates[0].shape, jnp.inf, jnp.float32))
    values = sort_values(values)
    return middle(values[len(values) // 2 - 1], values[len(values) // 2], fill)


def block_strips(block, at, tiles, height):
    parts = []
    for i in range(0, block_rows(tiles, height) // height, 2):
        pair = block[pl.ds(at + i * height, 2 * height), :].astype(jnp.float32)
        parts += [pair[:height], pair[height:]]
    return parts[:tiles], parts[tiles:]


def gather_candidates(block, at, targets, tiles):
    height, extent = targets[0].shape
    strips, ids = block_strips(block, at, tiles, height)
    found = [jnp.full((height, extent), jnp.inf, jnp.float32) for _ in targets]
    for t in range(tiles):
        row = t % height
        label = jnp.broadcast_to(ids[t // height][row : row + 1, :], (height, extent))
        for g, target in enumerate(targets):
            found[g] = jnp.where(label == target, strips[t], found[g])
    return found


def as_target(patch, shape):
    return jnp.full(shape, patch, jnp.int32).astype(jnp.float32)


def prep_kernel(
    patch_of, psf_weights, psf_basis, detect_taps, goals, cols, rows, weights, detect_cols, detect_rows
):
    n_targets, height, extent = goals.shape
    tiles = n_targets - 1
    rank, taps = psf_basis.shape[1:]
    shape = (height, extent)
    for t in range(tiles):
        goals[t] = as_target(patch_of[t], shape)
    goals[tiles] = as_target(lax.axis_index("visits"), shape)
    for q, reach in reaches(taps, extent):
        detect_cols[q] = col_tap_vector(detect_taps[1, q], reach, shape)
        for k in range(rank):
            cols[k, q] = col_tap_vector(psf_basis[1, k, q], reach, shape)
    for p, reach in reaches(taps, height):
        detect_rows[p] = row_tap_vector(detect_taps[0, p], reach, shape)
        for k in range(rank):
            rows[k, p] = row_tap_vector(psf_basis[0, k, p], reach, shape)
    for k in range(rank):
        for e in range(tiles):
            weights[k, e] = jnp.full(shape, psf_weights[1, k, e], jnp.float32)


def sift_kernel(block, goals, ranked, fills):
    n_targets, half, height, extent = ranked.shape
    targets = [goals[g] for g in range(n_targets)]
    rows_each = block.shape[0] // half
    for b in range(half):
        for g, value in enumerate(gather_candidates(block, b * rows_each, targets, n_targets - 1)):
            ranked[g, b] = value
    for g in range(n_targets):
        far = jnp.full((height, extent), jnp.inf, jnp.float32)
        values, fill = fill_missing([ranked[g, b] for b in range(half)], far)
        for b, value in enumerate(sort_values(values)):
            ranked[g, b] = value
        fills[g] = fill


def finish_kernel(
    block, warped, ranked, fills, goals, cols, rows, weights, detect_cols, detect_rows, *refs
):
    outputs, staged, sems, held = refs[:3], refs[3:6], refs[6], refs[7]
    template_out, difference_out, detection_out = staged
    copies = [pltpu.make_async_copy(staged[i], outputs[i], sems.at[i]) for i in range(3)]
    n_targets, half, _, _ = ranked.shape
    tiles = n_targets - 1
    rank, taps = cols.shape[:2]
    targets = [goals[g] for g in range(n_targets)]
    rows_each = block.shape[0] // half
    for b in range(half):
        for g, value in enumerate(gather_candidates(block, b * rows_each, targets, tiles)):
            held[g, b] = value
    models = []
    for g in range(n_targets):
        values, fill = fill_missing([held[g, b] for b in range(half)], fills[g])
        values = sort_values(values)
        lower, upper = None, None
        for b in range(half):
            first, second = ranked[g, b], values[half - 1 - b]
            low, high = jnp.minimum(first, second), jnp.maximum(first, second)
            lower = low if lower is None else jnp.maximum(lower, low)
            upper = high if upper is None else jnp.minimum(upper, high)
        models.append(middle(lower, upper, fill))
    template_out[0] = models[tiles].astype(jnp.bfloat16)
    copies[0].start()
    for first in range(0, tiles, CHUNK):
        chunk = range(first, min(first + CHUNK, tiles))
        modelled = tap_filter(
            [models[e] for e in chunk],
            rank,
            taps,
            lambda k, p, reach: rows[k, p],
            lambda k, q, reach: cols[k, q],
            lambda k, i, first=first: weights[k, first + i],
        )
        rest = []
        for i, e in enumerate(chunk):
            rest.append(jnp.where(targets[e] >= 0, warped[e] - modelled[i], 0.0))
            difference_out[e] = rest[-1]
        if chunk[-1] == tiles - 1:
            copies[1].start()
        detected = tap_filter(
            rest, 1, taps, lambda k, p, reach: detect_rows[p], lambda k, q, reach: detect_cols[q], None
        )
        for i, e in enumerate(chunk):
            detection_out[e] = detected[i]
    copies[2].start()
    for copy in copies:
        copy.wait()


def coadd_kernel(n_pieces, *refs):
    blocks = refs[:n_pieces]
    patch_of, psf_weights, psf_basis, detect_taps, warped = refs[n_pieces : n_pieces + 5]
    outputs = refs[n_pieces + 5 : n_pieces + 8]
    *staged, sems, held, models = refs[n_pieces + 8 :]
    template_out, difference_out, detection_out = staged
    copies = [pltpu.make_async_copy(staged[i], outputs[i], sems.at[i]) for i in range(3)]
    tiles, height, extent = warped.shape
    rank, taps = psf_basis.shape[1:]
    rows_each = block_rows(tiles, height)
    me = lax.axis_index("visits")
    visits = held.shape[0]

    def each_target(g, carry):
        patch = jnp.where(g < tiles, patch_of[jnp.minimum(g, tiles - 1)], me)
        target = [as_target(patch, (height, extent))]
        start = 0
        for block in blocks:

            def each_block(b, inner, block=block, start=start):
                at = pl.multiple_of(b * rows_each, 2 * height)
                held[start + b] = gather_candidates(block, at, target, tiles)[0]
                return inner

            count = block.shape[0] // rows_each
            lax.fori_loop(0, count, each_block, 0)
            start += count
        models[g] = median_of([held[s] for s in range(visits)])
        return carry

    lax.fori_loop(0, tiles + 1, each_target, 0)

    template_out[0] = models[tiles].astype(jnp.bfloat16)
    copies[0].start()
    for first in range(0, tiles, CHUNK):
        chunk = range(first, min(first + CHUNK, tiles))
        modelled = tap_filter(
            [models[e] for e in chunk],
            rank,
            taps,
            lambda k, p, reach: row_tap_vector(psf_basis[0, k, p], reach, (height, extent)),
            lambda k, q, reach: col_tap_vector(psf_basis[1, k, q], reach, (height, extent)),
            lambda k, i, first=first: psf_weights[1, k, first + i],
        )
        rest = []
        for i, e in enumerate(chunk):
            present = jnp.full((height, extent), patch_of[e], jnp.int32) >= 0
            rest.append(jnp.where(present, warped[e] - modelled[i], 0.0))
            difference_out[e] = rest[-1]
        if chunk[-1] == tiles - 1:
            copies[1].start()
        detected = tap_filter(
            rest,
            1,
            taps,
            lambda k, p, reach: row_tap_vector(detect_taps[0, p], reach, (height, extent)),
            lambda k, q, reach: col_tap_vector(detect_taps[1, q], reach, (height, extent)),
            None,
        )
        for i, e in enumerate(chunk):
            detection_out[e] = detected[i]
    copies[2].start()
    for copy in copies:
        copy.wait()


def gather_blocks(block, visits):
    if visits & (visits - 1):
        return [lax.all_gather(block, "visits", axis=0, tiled=True)]
    pieces = [block]
    for masks in exchange_stages(visits):
        held = pieces[0] if len(pieces) == 1 else jnp.concatenate(pieces, axis=0)
        pieces = [held]
        for mask in masks:
            partner = [(i, i ^ mask) for i in range(visits)]
            pieces.append(lax.ppermute(held, "visits", partner))
    return pieces


def exchange_stages(visits):
    bits = [1 << i for i in range(visits.bit_length() - 2, 0, -1)]
    stages = []
    while len(bits) > 2:
        stages.append([bits[0] ^ bits[1] | 1])
        bits = bits[1:]
    if len(bits) == 2:
        stages.append([bits[0] ^ bits[1] | 1, bits[1] | 1, bits[0] | 1])
    elif bits:
        stages.append([bits[0] | 1])
    return stages + [[1]] if visits > 1 else stages


def on_chip(value):
    if value.size > ON_CHIP_LIMIT:
        return value
    return pltpu.with_memory_space_constraint(value, pltpu.VMEM)


def shards(exposure, patch_of, affine, psf_weights, psf_basis, detect_taps):
    visits = lax.axis_size("visits")
    tiles, height, extent = exposure.shape
    if visits > 256 or visits & (visits - 1):
        raise ValueError("visits")
    vmem = pl.BlockSpec(memory_space=pltpu.VMEM)
    smem = pl.BlockSpec(memory_space=pltpu.SMEM)
    anywhere = pl.BlockSpec(memory_space=pl.ANY)
    rows = block_rows(tiles, height)
    warped, block = pl.pallas_call(
        match_kernel,
        name="match",
        out_shape=(
            pltpu.VMEM(exposure.shape, jnp.float32),
            pltpu.VMEM((rows, extent), jnp.bfloat16),
        ),
        in_specs=[vmem, smem, smem, smem, smem],
        out_specs=(vmem, vmem),
    )(exposure, patch_of, affine, psf_weights, psf_basis)
    pieces = [on_chip(piece) for piece in gather_blocks(block, visits)]
    warped = on_chip(warped)
    results = (
        jax.ShapeDtypeStruct((1, height, extent), jnp.bfloat16),
        jax.ShapeDtypeStruct(exposure.shape, jnp.float32),
        jax.ShapeDtypeStruct(exposure.shape, jnp.float32),
    )
    scratch = [pltpu.VMEM(result.shape, result.dtype) for result in results]
    scratch.append(pltpu.SemaphoreType.DMA((3,)))
    strip = (height, extent)
    if len(pieces) != 2 or visits * tiles * (tiles + 1) > UNROLL_LIMIT:
        return pl.pallas_call(
            lambda *refs: coadd_kernel(len(pieces), *refs),
            name="coadd",
            out_shape=results,
            in_specs=[vmem] * len(pieces) + [smem, smem, smem, smem, vmem],
            out_specs=(anywhere, anywhere, anywhere),
            scratch_shapes=scratch
            + [pltpu.VMEM((visits,) + strip, jnp.float32), pltpu.VMEM((tiles + 1,) + strip, jnp.float32)],
        )(*pieces, patch_of, psf_weights, psf_basis, detect_taps, warped)
    rank, taps = psf_basis.shape[1:]
    ranked_shape = (tiles + 1, visits // 2) + strip
    prepared = pl.pallas_call(
        prep_kernel,
        name="prep",
        out_shape=tuple(
            pltpu.VMEM(shape + strip, jnp.float32)
            for shape in ((tiles + 1,), (rank, taps), (rank, taps), (rank, tiles), (taps,), (taps,))
        ),
        in_specs=[smem] * 4,
        out_specs=(vmem,) * 6,
    )(patch_of, psf_weights, psf_basis, detect_taps)
    prepared = [on_chip(value) for value in prepared]
    sifted = pl.pallas_call(
        sift_kernel,
        name="sift",
        out_shape=(pltpu.VMEM(ranked_shape, jnp.float32), pltpu.VMEM((tiles + 1,) + strip, jnp.float32)),
        in_specs=[vmem] * 2,
        out_specs=(vmem,) * 2,
    )(pieces[0], prepared[0])
    return pl.pallas_call(
        finish_kernel,
        name="finish",
        out_shape=results,
        in_specs=[vmem] * 10,
        out_specs=(anywhere, anywhere, anywhere),
        scratch_shapes=scratch + [pltpu.VMEM(ranked_shape, jnp.float32)],
    )(pieces[1], warped, *[on_chip(value) for value in sifted], *prepared)


def solution(mesh):
    placed = (
        P(("groups", "visits"), None, None),
        P(("groups", "visits")),
        P(None, ("groups", "visits")),
        P(None, None, ("groups", "visits")),
        P(),
        P(),
    )

    return jax.shard_map(
        shards,
        mesh=mesh,
        in_specs=placed,
        out_specs=(
            P(("groups", "visits"), None, None),
            P(("groups", "visits"), None, None),
            P(("groups", "visits"), None, None),
        ),
        check_vma=False,
    )
```

profile of v0, /device:TPU:0, one launch (start us, length us, event | category | flops | bytes accessed | tf_op | source)
XLA Modules:
  0.0 17.7 jit_solution(334788429321953820)
XLA Ops:
  0.6 1.5 %match.1 = (f32[7,8,128]{2,1,0:T(8,128)S(1)}, bf16[64,128]{1,0:T(8,128)(2,1)S(1)}) custom-call(f32[7,8,128]{2,1,0:T(8,128)} %exposure.1, s32[7]{0:T(128)} %patch_of.3, s32[6,7]{1,0:T(8,128)} %affine.1, f32[2,4,7]{2,1,0:T(4,128)} %psf_weights.3, f32[2,4,21]{2,1,0:T(4,128)} %psf_basis.3), custom_call_target="tpu_custom_call" | custom-call | tf_op jit(solution)/shard_map/match/pallas_call | solution.py:375
  2.2 4.6 %collective-permute-start = (bf16[64,128]{1,0:T(8,128)(2,1)S(1)}, bf16[64,128]{1,0:T(8,128)(2,1)S(1)}, u32[]{:S(2)}, u32[]{:S(2)}) collective-permute-start(bf16[64,128]{1,0:T(8,128)(2,1)S(1)} %get-tuple-element.13), channel_id=1, source_target_pairs={{0,13},{1,12},{2,15},{3,14},{4,9},{5,8},{6,11},{7,10},{8,5},{9,4},... | collective-permute-start | bytes 49160 | tf_op jit(solution)/shard_map/ppermute | solution.py:343
  6.8 1.5 %collective-permute-done = bf16[64,128]{1,0:T(8,128)(2,1)S(1)} collective-permute-done((bf16[64,128]{1,0:T(8,128)(2,1)S(1)}, bf16[64,128]{1,0:T(8,128)(2,1)S(1)}, u32[]{:S(2)}, u32[]{:S(2)}) %collective-permute-start) | collective-permute-done | bytes 16416 | tf_op jit(solution)/shard_map/ppermute | solution.py:343
  8.2 1.0 %collective-permute-start.1 = (bf16[128,128]{1,0:T(8,128)(2,1)S(1)}, bf16[128,128]{1,0:T(8,128)(2,1)S(1)}, u32[]{:S(2)}, u32[]{:S(2)}) collective-permute-start(bf16[128,128]{1,0:T(8,128)(2,1)S(1)} %get-tuple-element.23), channel_id=1, source_target_pairs={{0,7},{1,6},{2,5},{3,4},{4,3},{5,2},{6,1},{7,0},{8,15},{9,14},{10,... | collective-permute-start | bytes 98312 | tf_op jit(solution)/shard_map/ppermute | solution.py:343
  9.2 2.2 %collective-permute-start.3 = (bf16[128,128]{1,0:T(8,128)(2,1)S(1)}, bf16[128,128]{1,0:T(8,128)(2,1)S(1)}, u32[]{:S(2)}, u32[]{:S(2)}) collective-permute-start(bf16[128,128]{1,0:T(8,128)(2,1)S(1)} %get-tuple-element.23), channel_id=1, source_target_pairs={{0,5},{1,4},{2,7},{3,6},{4,1},{5,0},{6,3},{7,2},{8,13},{9,12},{10,... | collective-permute-start | bytes 98312 | tf_op jit(solution)/shard_map/ppermute | solution.py:343
  11.4 0.3 %collective-permute-start.2 = (bf16[128,128]{1,0:T(8,128)(2,1)S(1)}, bf16[128,128]{1,0:T(8,128)(2,1)S(1)}, u32[]{:S(2)}, u32[]{:S(2)}) collective-permute-start(bf16[128,128]{1,0:T(8,128)(2,1)S(1)} %get-tuple-element.23), channel_id=1, source_target_pairs={{0,3},{1,2},{2,1},{3,0},{4,7},{5,6},{6,5},{7,4},{8,11},{9,10},{10,... | collective-permute-start | bytes 98312 | tf_op jit(solution)/shard_map/ppermute | solution.py:343
  11.7 0.8 %collective-permute-done.1 = bf16[128,128]{1,0:T(8,128)(2,1)S(1)} collective-permute-done((bf16[128,128]{1,0:T(8,128)(2,1)S(1)}, bf16[128,128]{1,0:T(8,128)(2,1)S(1)}, u32[]{:S(2)}, u32[]{:S(2)}) %collective-permute-start.1) | collective-permute-done | bytes 32800 | tf_op jit(solution)/shard_map/ppermute | solution.py:343
  12.6 2.2 %collective-permute-done.2 = bf16[128,128]{1,0:T(8,128)(2,1)S(1)} collective-permute-done((bf16[128,128]{1,0:T(8,128)(2,1)S(1)}, bf16[128,128]{1,0:T(8,128)(2,1)S(1)}, u32[]{:S(2)}, u32[]{:S(2)}) %collective-permute-start.2) | collective-permute-done | bytes 32800 | tf_op jit(solution)/shard_map/ppermute | solution.py:343
  14.8 0.0 collective-permute-done.3
  14.8 0.2 %collective-permute-start.4 = (bf16[512,128]{1,0:T(8,128)(2,1)S(1)}, bf16[512,128]{1,0:T(8,128)(2,1)S(1)}, u32[]{:S(2)}, u32[]{:S(2)}) collective-permute-start(bf16[512,128]{1,0:T(8,128)(2,1)S(1)} %constant_dynamic-update-slice_fusion.2.block), channel_id=1, source_target_pairs={{0,1},{1,0},{2,3},{3,2},{4,5},{5,4},{6,7},{7,6},{8,9},{9,8},{10,11... | collective-permute-start | bytes 393224 | tf_op jit(solution)/shard_map/ppermute | solution.py:343
  15.0 0.9 %prep.1 = (f32[8,8,128]{2,1,0:T(8,128)S(1)}, f32[4,21,8,128]{3,2,1,0:T(8,128)S(1)}, f32[4,21,8,128]{3,2,1,0:T(8,128)S(1)}, f32[4,7,8,128]{3,2,1,0:T(8,128)S(1)},...) custom-call(s32[7]{0:T(128)} %patch_of.3, f32[2,4,7]{2,1,0:T(4,128)} %psf_weights.3, f32[2,4,21]{2,1,0:T(4,128)} %psf_basis.3, ...), custom_call_target="tpu_custom_call" | custom-call | tf_op jit(solution)/shard_map/prep/pallas_call | solution.py:407
  15.9 0.2 %sift.1 = (f32[8,8,8,128]{3,2,1,0:T(8,128)S(1)}, f32[8,8,128]{2,1,0:T(8,128)S(1)}) custom-call(bf16[512,128]{1,0:T(8,128)(2,1)S(1)} %constant_dynamic-update-slice_fusion.2.block, f32[8,8,128]{2,1,0:T(8,128)S(1)} %get-tuple-element.15.goals), custom_call_target="tpu_custom_call" | custom-call | tf_op jit(solution)/shard_map/sift/pallas_call | solution.py:418
  16.2 0.0 collective-permute-done.4.block
  16.2 1.5 %finish.1 = (bf16[1,8,128]{2,1,0:T(8,128)(2,1)}, f32[7,8,128]{2,1,0:T(8,128)}, f32[7,8,128]{2,1,0:T(8,128)}) custom-call(bf16[512,128]{1,0:T(8,128)(2,1)S(1)} %collective-permute-done.4.block, f32[7,8,128]{2,1,0:T(8,128)S(1)} %get-tuple-element.14.warped, f32[8,8,8,128]{3,2,1,0:T(8,128)S(1)} %get-tuple-element.16.ranked, ...), custom_call_target="tpu_custom_call" | custom-call | tf_op jit(solution)/shard_map/finish/pallas_call | solution.py:425
  (5 shorter events, 0.0 us)
Async XLA Ops:
  2.2 6.1 %collective-permute-start = (bf16[64,128]{1,0:T(8,128)(2,1)S(1)}, bf16[64,128]{1,0:T(8,128)(2,1)S(1)}, u32[]{:S(2)}, u32[]{:S(2)}) collective-permute-start(bf16[64,128]{1,0:T(8,128)(2,1)S(1)} %get-tuple-element.13), channel_id=1, source_target_pairs={{0,13},{1,12},{2,15},{3,14},{4,9},{5,8},{6,11},{7,10},{8,5},{9,4},... | collective-permute-start | bytes 49160 | tf_op jit(solution)/shard_map/ppermute | solution.py:343
  8.2 4.3 %collective-permute-start.1 = (bf16[128,128]{1,0:T(8,128)(2,1)S(1)}, bf16[128,128]{1,0:T(8,128)(2,1)S(1)}, u32[]{:S(2)}, u32[]{:S(2)}) collective-permute-start(bf16[128,128]{1,0:T(8,128)(2,1)S(1)} %get-tuple-element.23), channel_id=1, source_target_pairs={{0,7},{1,6},{2,5},{3,4},{4,3},{5,2},{6,1},{7,0},{8,15},{9,14},{10,... | collective-permute-start | bytes 98312 | tf_op jit(solution)/shard_map/ppermute | solution.py:343
  9.2 5.6 %collective-permute-start.3 = (bf16[128,128]{1,0:T(8,128)(2,1)S(1)}, bf16[128,128]{1,0:T(8,128)(2,1)S(1)}, u32[]{:S(2)}, u32[]{:S(2)}) collective-permute-start(bf16[128,128]{1,0:T(8,128)(2,1)S(1)} %get-tuple-element.23), channel_id=1, source_target_pairs={{0,5},{1,4},{2,7},{3,6},{4,1},{5,0},{6,3},{7,2},{8,13},{9,12},{10,... | collective-permute-start | bytes 98312 | tf_op jit(solution)/shard_map/ppermute | solution.py:343
  11.4 3.3 %collective-permute-start.2 = (bf16[128,128]{1,0:T(8,128)(2,1)S(1)}, bf16[128,128]{1,0:T(8,128)(2,1)S(1)}, u32[]{:S(2)}, u32[]{:S(2)}) collective-permute-start(bf16[128,128]{1,0:T(8,128)(2,1)S(1)} %get-tuple-element.23), channel_id=1, source_target_pairs={{0,3},{1,2},{2,1},{3,0},{4,7},{5,6},{6,5},{7,4},{8,11},{9,10},{10,... | collective-permute-start | bytes 98312 | tf_op jit(solution)/shard_map/ppermute | solution.py:343
  14.8 1.4 %collective-permute-start.4 = (bf16[512,128]{1,0:T(8,128)(2,1)S(1)}, bf16[512,128]{1,0:T(8,128)(2,1)S(1)}, u32[]{:S(2)}, u32[]{:S(2)}) collective-permute-start(bf16[512,128]{1,0:T(8,128)(2,1)S(1)} %constant_dynamic-update-slice_fusion.2.block), channel_id=1, source_target_pairs={{0,1},{1,0},{2,3},{3,2},{4,5},{5,4},{6,7},{7,6},{8,9},{9,8},{10,11... | collective-permute-start | bytes 393224 | tf_op jit(solution)/shard_map/ppermute | solution.py:343
where the time goes:
time: 17.9 us; the launch traced here: 17.7 us
  starting transfers between devices  8.31 us (46%)
  waiting for transfers between devices  4.54 us (25%)
  Pallas kernels  4.13 us (23%)
  between operations  0.66 us (4%)
    ppermute x5, starting transfers between devices, gather_blocks(): pieces.append(lax.ppermute(held, 'visits', partner))  8.31 us
    ppermute x5, waiting for transfers between devices, gather_blocks(): pieces.append(lax.ppermute(held, 'visits', partner))  4.54 us
    pallas_call x1, Pallas kernels, shards(): pl.pallas_call(match_kernel, name='match', out_shape=(pltpu.VMEM(exposure...  1.53 us
    pallas_call x1, Pallas kernels, shards(): pl.pallas_call(finish_kernel, name='finish', out_shape=results, in_specs=...  1.48 us
    pallas_call x1, Pallas kernels, shards(): pl.pallas_call(prep_kernel, name='prep', out_shape=tuple((pltpu.VMEM(shap...  0.89 us
  transfers between devices with their start and end apart: 5, of which 3 were waited for; matrix products, arithmetic and copies ran while one was open for 0% of the time, Pallas kernels for 6%

commit v1 on v0

--- a/solution.py
+++ b/solution.py
@@ -75,32 +75,45 @@
     return warped
 
 
-def match_kernel(exposure, patch_of, affine, psf_weights, psf_basis, warped_out, block_out):
+def match_kernel(*refs):
+    sources, (warped_out, block_out), (sems, *held) = refs[:5], refs[5:7], refs[7:]
+    copies = [pltpu.make_async_copy(sources[i], held[i], sems.at[i]) for i in range(5)]
+    exposure, affine, psf_basis, psf_weights, patch_of = held
+    for copy in copies:
+        copy.start()
     tiles, height, extent = exposure.shape
     rank, taps = psf_basis.shape[1:]
+    shape = (height, extent)
     pieces = []
     for first in range(0, tiles, CHUNK):
         chunk = range(first, min(first + CHUNK, tiles))
+        if first == 0:
+            copies[0].wait()
+            copies[1].wait()
         strips = []
         for e in chunk:
             strips.append(warp_strip(exposure[e], lambda row, e=e: affine[row, e]))
             warped_out[e] = strips[-1]
+        if first == 0:
+            copies[2].wait()
+            copies[3].wait()
         pieces += tap_filter(
             strips,
             rank,
             taps,
-            lambda k, p, reach: row_tap_vector(psf_basis[0, k, p], reach, (height, extent)),
-            lambda k, q, reach: col_tap_vector(psf_basis[1, k, q], reach, (height, extent)),
+            lambda k, p, reach: row_tap_vector(psf_basis[0, k, p], reach, shape),
+            lambda k, q, reach: col_tap_vector(psf_basis[1, k, q], reach, shape),
             lambda k, i, first=first: psf_weights[0, k, first + i],
         )
-    rows = lax.broadcasted_iota(jnp.int32, (height, extent), 0)
+    copies[4].wait()
+    rows = lax.broadcasted_iota(jnp.int32, shape, 0)
     for first in range(0, tiles, height):
-        ids = jnp.full((height, extent), -1, jnp.int32)
+        ids = jnp.full(shape, -1, jnp.int32)
         for t in range(first, min(first + height, tiles)):
             ids = jnp.where(rows == t - first, patch_of[t], ids)
         pieces.append(ids.astype(jnp.float32))
     while len(pieces) * height < block_out.shape[0]:
-        pieces.append(jnp.full((height, extent), -1.0, jnp.float32))
+        pieces.append(jnp.full(shape, -1.0, jnp.float32))
     for i in range(0, len(pieces), 2):
         pair = jnp.concatenate(pieces[i : i + 2], axis=0)
         block_out[i * height : (i + 2) * height, :] = pair.astype(jnp.bfloat16)
@@ -379,9 +392,14 @@
             pltpu.VMEM(exposure.shape, jnp.float32),
             pltpu.VMEM((rows, extent), jnp.bfloat16),
         ),
-        in_specs=[vmem, smem, smem, smem, smem],
+        in_specs=[anywhere] * 5,
         out_specs=(vmem, vmem),
-    )(exposure, patch_of, affine, psf_weights, psf_basis)
+        scratch_shapes=[
+            pltpu.SemaphoreType.DMA((5,)),
+            pltpu.VMEM(exposure.shape, exposure.dtype),
+            *(pltpu.SMEM(value.shape, value.dtype) for value in (affine, psf_basis, psf_weights, patch_of)),
+        ],
+    )(exposure, affine, psf_basis, psf_weights, patch_of)
     pieces = [on_chip(piece) for piece in gather_blocks(block, visits)]
     warped = on_chip(warped)
     results = (

time: 17.9 us -> 17.8 us (level)
  no operation moved by 1% of the time
where the time goes in v1:
time: 17.8 us; the launch traced here: 17.6 us
  starting transfers between devices  8.31 us (47%)
  waiting for transfers between devices  4.54 us (26%)
  Pallas kernels  4.07 us (23%)
  between operations  0.66 us (4%)
    ppermute x5, starting transfers between devices, gather_blocks(): pieces.append(lax.ppermute(held, 'visits', partner))  8.31 us
    ppermute x5, waiting for transfers between devices, gather_blocks(): pieces.append(lax.ppermute(held, 'visits', partner))  4.54 us
    pallas_call x1, Pallas kernels, shards(): pl.pallas_call(finish_kernel, name='finish', out_shape=results, in_specs=...  1.48 us
    pallas_call x1, Pallas kernels, shards(): pl.pallas_call(match_kernel, name='match', out_shape=(pltpu.VMEM(exposure...  1.47 us
    pallas_call x1, Pallas kernels, shards(): pl.pallas_call(prep_kernel, name='prep', out_shape=tuple((pltpu.VMEM(shap...  0.89 us
  transfers between devices with their start and end apart: 5, of which 3 were waited for; matrix products, arithmetic and copies ran while one was open for 0% of the time, Pallas kernels for 6%

profile of v1, /device:TPU:0, one launch (start us, length us, event | category | flops | bytes accessed | tf_op | source)
XLA Modules:
  0.0 17.6 jit_solution(9361873269154931066)
XLA Ops:
  0.6 1.5 %match.1 = (f32[7,8,128]{2,1,0:T(8,128)S(1)}, bf16[64,128]{1,0:T(8,128)(2,1)S(1)}) custom-call(f32[7,8,128]{2,1,0:T(8,128)} %refs_0_.1, s32[6,7]{1,0:T(8,128)} %refs_1_.1, f32[2,4,21]{2,1,0:T(4,128)} %psf_basis.1, f32[2,4,7]{2,1,0:T(4,128)} %psf_weights.1, s32[7]{0:T(128)} %patch_of.1), custom_call_target="tpu_custom_call" | custom-call | tf_op jit(solution)/shard_map/match/pallas_call | solution.py:388
  2.1 4.6 %collective-permute-start = (bf16[64,128]{1,0:T(8,128)(2,1)S(1)}, bf16[64,128]{1,0:T(8,128)(2,1)S(1)}, u32[]{:S(2)}, u32[]{:S(2)}) collective-permute-start(bf16[64,128]{1,0:T(8,128)(2,1)S(1)} %get-tuple-element.13), channel_id=1, source_target_pairs={{0,13},{1,12},{2,15},{3,14},{4,9},{5,8},{6,11},{7,10},{8,5},{9,4},... | collective-permute-start | bytes 49160 | tf_op jit(solution)/shard_map/ppermute | solution.py:356
  6.7 1.5 %collective-permute-done = bf16[64,128]{1,0:T(8,128)(2,1)S(1)} collective-permute-done((bf16[64,128]{1,0:T(8,128)(2,1)S(1)}, bf16[64,128]{1,0:T(8,128)(2,1)S(1)}, u32[]{:S(2)}, u32[]{:S(2)}) %collective-permute-start) | collective-permute-done | bytes 16416 | tf_op jit(solution)/shard_map/ppermute | solution.py:356
  8.2 1.0 %collective-permute-start.1 = (bf16[128,128]{1,0:T(8,128)(2,1)S(1)}, bf16[128,128]{1,0:T(8,128)(2,1)S(1)}, u32[]{:S(2)}, u32[]{:S(2)}) collective-permute-start(bf16[128,128]{1,0:T(8,128)(2,1)S(1)} %get-tuple-element.23), channel_id=1, source_target_pairs={{0,7},{1,6},{2,5},{3,4},{4,3},{5,2},{6,1},{7,0},{8,15},{9,14},{10,... | collective-permute-start | bytes 98312 | tf_op jit(solution)/shard_map/ppermute | solution.py:356
  9.2 2.2 %collective-permute-start.3 = (bf16[128,128]{1,0:T(8,128)(2,1)S(1)}, bf16[128,128]{1,0:T(8,128)(2,1)S(1)}, u32[]{:S(2)}, u32[]{:S(2)}) collective-permute-start(bf16[128,128]{1,0:T(8,128)(2,1)S(1)} %get-tuple-element.23), channel_id=1, source_target_pairs={{0,5},{1,4},{2,7},{3,6},{4,1},{5,0},{6,3},{7,2},{8,13},{9,12},{10,... | collective-permute-start | bytes 98312 | tf_op jit(solution)/shard_map/ppermute | solution.py:356
  11.4 0.3 %collective-permute-start.2 = (bf16[128,128]{1,0:T(8,128)(2,1)S(1)}, bf16[128,128]{1,0:T(8,128)(2,1)S(1)}, u32[]{:S(2)}, u32[]{:S(2)}) collective-permute-start(bf16[128,128]{1,0:T(8,128)(2,1)S(1)} %get-tuple-element.23), channel_id=1, source_target_pairs={{0,3},{1,2},{2,1},{3,0},{4,7},{5,6},{6,5},{7,4},{8,11},{9,10},{10,... | collective-permute-start | bytes 98312 | tf_op jit(solution)/shard_map/ppermute | solution.py:356
  11.7 0.8 %collective-permute-done.1 = bf16[128,128]{1,0:T(8,128)(2,1)S(1)} collective-permute-done((bf16[128,128]{1,0:T(8,128)(2,1)S(1)}, bf16[128,128]{1,0:T(8,128)(2,1)S(1)}, u32[]{:S(2)}, u32[]{:S(2)}) %collective-permute-start.1) | collective-permute-done | bytes 32800 | tf_op jit(solution)/shard_map/ppermute | solution.py:356
  12.5 2.2 %collective-permute-done.2 = bf16[128,128]{1,0:T(8,128)(2,1)S(1)} collective-permute-done((bf16[128,128]{1,0:T(8,128)(2,1)S(1)}, bf16[128,128]{1,0:T(8,128)(2,1)S(1)}, u32[]{:S(2)}, u32[]{:S(2)}) %collective-permute-start.2) | collective-permute-done | bytes 32800 | tf_op jit(solution)/shard_map/ppermute | solution.py:356
  14.7 0.0 collective-permute-done.3
  14.7 0.2 %collective-permute-start.4 = (bf16[512,128]{1,0:T(8,128)(2,1)S(1)}, bf16[512,128]{1,0:T(8,128)(2,1)S(1)}, u32[]{:S(2)}, u32[]{:S(2)}) collective-permute-start(bf16[512,128]{1,0:T(8,128)(2,1)S(1)} %constant_dynamic-update-slice_fusion.2.block), channel_id=1, source_target_pairs={{0,1},{1,0},{2,3},{3,2},{4,5},{5,4},{6,7},{7,6},{8,9},{9,8},{10,11... | collective-permute-start | bytes 393224 | tf_op jit(solution)/shard_map/ppermute | solution.py:356
  15.0 0.9 %prep.1 = (f32[8,8,128]{2,1,0:T(8,128)S(1)}, f32[4,21,8,128]{3,2,1,0:T(8,128)S(1)}, f32[4,21,8,128]{3,2,1,0:T(8,128)S(1)}, f32[4,7,8,128]{3,2,1,0:T(8,128)S(1)},...) custom-call(s32[7]{0:T(128)} %patch_of.1, f32[2,4,7]{2,1,0:T(4,128)} %psf_weights.1, f32[2,4,21]{2,1,0:T(4,128)} %psf_basis.1, ...), custom_call_target="tpu_custom_call" | custom-call | tf_op jit(solution)/shard_map/prep/pallas_call | solution.py:425
  15.9 0.2 %sift.1 = (f32[8,8,8,128]{3,2,1,0:T(8,128)S(1)}, f32[8,8,128]{2,1,0:T(8,128)S(1)}) custom-call(bf16[512,128]{1,0:T(8,128)(2,1)S(1)} %constant_dynamic-update-slice_fusion.2.block, f32[8,8,128]{2,1,0:T(8,128)S(1)} %get-tuple-element.15.goals), custom_call_target="tpu_custom_call" | custom-call | tf_op jit(solution)/shard_map/sift/pallas_call | solution.py:436
  16.1 0.0 collective-permute-done.4.block
  16.1 1.5 %finish.1 = (bf16[1,8,128]{2,1,0:T(8,128)(2,1)}, f32[7,8,128]{2,1,0:T(8,128)}, f32[7,8,128]{2,1,0:T(8,128)}) custom-call(bf16[512,128]{1,0:T(8,128)(2,1)S(1)} %collective-permute-done.4.block, f32[7,8,128]{2,1,0:T(8,128)S(1)} %get-tuple-element.14.warped, f32[8,8,8,128]{3,2,1,0:T(8,128)S(1)} %get-tuple-element.16.ranked, ...), custom_call_target="tpu_custom_call" | custom-call | tf_op jit(solution)/shard_map/finish/pallas_call | solution.py:443
  (5 shorter events, 0.0 us)
Async XLA Ops:
  2.1 6.1 %collective-permute-start = (bf16[64,128]{1,0:T(8,128)(2,1)S(1)}, bf16[64,128]{1,0:T(8,128)(2,1)S(1)}, u32[]{:S(2)}, u32[]{:S(2)}) collective-permute-start(bf16[64,128]{1,0:T(8,128)(2,1)S(1)} %get-tuple-element.13), channel_id=1, source_target_pairs={{0,13},{1,12},{2,15},{3,14},{4,9},{5,8},{6,11},{7,10},{8,5},{9,4},... | collective-permute-start | bytes 49160 | tf_op jit(solution)/shard_map/ppermute | solution.py:356
  8.2 4.3 %collective-permute-start.1 = (bf16[128,128]{1,0:T(8,128)(2,1)S(1)}, bf16[128,128]{1,0:T(8,128)(2,1)S(1)}, u32[]{:S(2)}, u32[]{:S(2)}) collective-permute-start(bf16[128,128]{1,0:T(8,128)(2,1)S(1)} %get-tuple-element.23), channel_id=1, source_target_pairs={{0,7},{1,6},{2,5},{3,4},{4,3},{5,2},{6,1},{7,0},{8,15},{9,14},{10,... | collective-permute-start | bytes 98312 | tf_op jit(solution)/shard_map/ppermute | solution.py:356
  9.2 5.6 %collective-permute-start.3 = (bf16[128,128]{1,0:T(8,128)(2,1)S(1)}, bf16[128,128]{1,0:T(8,128)(2,1)S(1)}, u32[]{:S(2)}, u32[]{:S(2)}) collective-permute-start(bf16[128,128]{1,0:T(8,128)(2,1)S(1)} %get-tuple-element.23), channel_id=1, source_target_pairs={{0,5},{1,4},{2,7},{3,6},{4,1},{5,0},{6,3},{7,2},{8,13},{9,12},{10,... | collective-permute-start | bytes 98312 | tf_op jit(solution)/shard_map/ppermute | solution.py:356
  11.4 3.3 %collective-permute-start.2 = (bf16[128,128]{1,0:T(8,128)(2,1)S(1)}, bf16[128,128]{1,0:T(8,128)(2,1)S(1)}, u32[]{:S(2)}, u32[]{:S(2)}) collective-permute-start(bf16[128,128]{1,0:T(8,128)(2,1)S(1)} %get-tuple-element.23), channel_id=1, source_target_pairs={{0,3},{1,2},{2,1},{3,0},{4,7},{5,6},{6,5},{7,4},{8,11},{9,10},{10,... | collective-permute-start | bytes 98312 | tf_op jit(solution)/shard_map/ppermute | solution.py:356
  14.7 1.4 %collective-permute-start.4 = (bf16[512,128]{1,0:T(8,128)(2,1)S(1)}, bf16[512,128]{1,0:T(8,128)(2,1)S(1)}, u32[]{:S(2)}, u32[]{:S(2)}) collective-permute-start(bf16[512,128]{1,0:T(8,128)(2,1)S(1)} %constant_dynamic-update-slice_fusion.2.block), channel_id=1, source_target_pairs={{0,1},{1,0},{2,3},{3,2},{4,5},{5,4},{6,7},{7,6},{8,9},{9,8},{10,11... | collective-permute-start | bytes 393224 | tf_op jit(solution)/shard_map/ppermute | solution.py:356

commit v2 on v1

--- a/solution.py
+++ b/solution.py
@@ -37,7 +37,7 @@
 
 
 def tap_filter(strips, rank, taps, row_tap, col_tap, weight):
-    height, extent = strips[0].shape
+    _, extent = strips[0].shape
     partial = [[None] * rank for _ in strips]
     for q, reach in reaches(taps, extent):
         scale = [col_tap(k, q, reach) for k in range(rank)]
@@ -46,12 +46,17 @@
             for k in range(rank):
                 term = scale[k] * moved
                 partial[e][k] = term if partial[e][k] is None else partial[e][k] + term
+    return mix_rows(partial, rank, taps, row_tap, weight)
+
+
+def mix_rows(partial, rank, taps, row_tap, weight):
+    height = partial[0][0].shape[0]
     if weight is not None:
-        partial = [[weight(k, e) * partial[e][k] for k in range(rank)] for e in range(len(strips))]
-    totals = [None] * len(strips)
+        partial = [[weight(k, e) * partial[e][k] for k in range(rank)] for e in range(len(partial))]
+    totals = [None] * len(partial)
     for p, reach in reaches(taps, height):
         scale = [row_tap(k, p, reach) for k in range(rank)]
-        for e in range(len(strips)):
+        for e in range(len(partial)):
             mixed = scale[0] * partial[e][0]
             for k in range(1, rank):
                 mixed = mixed + scale[k] * partial[e][k]
@@ -187,8 +192,33 @@
     return jnp.full(shape, patch, jnp.int32).astype(jnp.float32)
 
 
+def store_bands(bands, rank, taps, shape, tap):
+    height, extent = shape
+    row = lax.broadcasted_iota(jnp.int32, shape, 0)
+    col = lax.broadcasted_iota(jnp.int32, shape, 1)
+    centre = (taps - 1) // 2
+    offset = row - col
+    offset = jnp.where(offset < -centre, offset + extent, offset)
+    heads = [jnp.zeros(shape, jnp.float32) for _ in range(rank)]
+    for q, reach in reaches(taps, extent):
+        here = offset == reach
+        heads = [jnp.where(here, tap(k, q), heads[k]) for k in range(rank)]
+    for at in range(0, extent, 2 * height):
+        for k in range(rank):
+            parts = []
+            for top in (at, at + height):
+                moved = pltpu.roll(heads[k], top, 1) if top else heads[k]
+                parts.append(jnp.where(jnp.abs(row + top - col) <= centre, moved, 0.0))
+            value = jnp.concatenate(parts, axis=0)
+            high = value.astype(jnp.bfloat16)
+            low = (value - high.astype(jnp.float32)).astype(jnp.bfloat16)
+            lanes = slice(k * extent, (k + 1) * extent)
+            bands[at : at + 2 * height, lanes] = high
+            bands[extent + at : extent + at + 2 * height, lanes] = low
+
+
 def prep_kernel(
-    patch_of, psf_weights, psf_basis, detect_taps, goals, cols, rows, weights, detect_cols, detect_rows
+    patch_of, psf_weights, psf_basis, detect_taps, goals, bands, rows, weights, detect_cols, detect_rows
 ):
     n_targets, height, extent = goals.shape
     tiles = n_targets - 1
@@ -199,8 +229,7 @@
     goals[tiles] = as_target(lax.axis_index("visits"), shape)
     for q, reach in reaches(taps, extent):
         detect_cols[q] = col_tap_vector(detect_taps[1, q], reach, shape)
-        for k in range(rank):
-            cols[k, q] = col_tap_vector(psf_basis[1, k, q], reach, shape)
+    store_bands(bands, rank, taps, shape, lambda k, q: psf_basis[1, k, q])
     for p, reach in reaches(taps, height):
         detect_rows[p] = row_tap_vector(detect_taps[0, p], reach, shape)
         for k in range(rank):
@@ -226,14 +255,14 @@
 
 
 def finish_kernel(
-    block, warped, ranked, fills, goals, cols, rows, weights, detect_cols, detect_rows, *refs
+    block, warped, ranked, fills, goals, bands, rows, weights, detect_cols, detect_rows, *refs
 ):
     outputs, staged, sems, held = refs[:3], refs[3:6], refs[6], refs[7]
     template_out, difference_out, detection_out = staged
     copies = [pltpu.make_async_copy(staged[i], outputs[i], sems.at[i]) for i in range(3)]
-    n_targets, half, _, _ = ranked.shape
+    n_targets, half, height, extent = ranked.shape
     tiles = n_targets - 1
-    rank, taps = cols.shape[:2]
+    rank, taps = rows.shape[:2]
     targets = [goals[g] for g in range(n_targets)]
     rows_each = block.shape[0] // half
     for b in range(half):
@@ -252,27 +281,26 @@
         models.append(middle(lower, upper, fill))
     template_out[0] = models[tiles].astype(jnp.bfloat16)
     copies[0].start()
-    for first in range(0, tiles, CHUNK):
-        chunk = range(first, min(first + CHUNK, tiles))
-        modelled = tap_filter(
-            [models[e] for e in chunk],
-            rank,
-            taps,
-            lambda k, p, reach: rows[k, p],
-            lambda k, q, reach: cols[k, q],
-            lambda k, i, first=first: weights[k, first + i],
-        )
-        rest = []
-        for i, e in enumerate(chunk):
-            rest.append(jnp.where(targets[e] >= 0, warped[e] - modelled[i], 0.0))
-            difference_out[e] = rest[-1]
-        if chunk[-1] == tiles - 1:
-            copies[1].start()
-        detected = tap_filter(
-            rest, 1, taps, lambda k, p, reach: detect_rows[p], lambda k, q, reach: detect_cols[q], None
-        )
-        for i, e in enumerate(chunk):
-            detection_out[e] = detected[i]
+    stack = models + [jnp.zeros((height, extent), jnp.float32)] * (n_targets % 2)
+    stack = jnp.concatenate(stack, axis=0).astype(jnp.bfloat16)
+    spread = jnp.dot(
+        jnp.concatenate([stack, stack], axis=1), bands[...], preferred_element_type=jnp.float32
+    )
+    partial = [
+        [spread[e * height : (e + 1) * height, k * extent : (k + 1) * extent] for k in range(rank)]
+        for e in range(tiles)
+    ]
+    modelled = mix_rows(partial, rank, taps, lambda k, p, reach: rows[k, p], lambda k, e: weights[k, e])
+    rest = []
+    for e in range(tiles):
+        rest.append(jnp.where(targets[e] >= 0, warped[e] - modelled[e], 0.0))
+        difference_out[e] = rest[-1]
+    copies[1].start()
+    detected = tap_filter(
+        rest, 1, taps, lambda k, p, reach: detect_rows[p], lambda k, q, reach: detect_cols[q], None
+    )
+    for e in range(tiles):
+        detection_out[e] = detected[e]
     copies[2].start()
     for copy in copies:
         copy.wait()
@@ -426,8 +454,15 @@
         prep_kernel,
         name="prep",
         out_shape=tuple(
-            pltpu.VMEM(shape + strip, jnp.float32)
-            for shape in ((tiles + 1,), (rank, taps), (rank, taps), (rank, tiles), (taps,), (taps,))
+            pltpu.VMEM(shape, dtype)
+            for shape, dtype in (
+                ((tiles + 1,) + strip, jnp.float32),
+                ((2 * extent, rank * extent), jnp.bfloat16),
+                ((rank, taps) + strip, jnp.float32),
+                ((rank, tiles) + strip, jnp.float32),
+                ((taps,) + strip, jnp.float32),
+                ((taps,) + strip, jnp.float32),
+            )
         ),
         in_specs=[smem] * 4,
         out_specs=(vmem,) * 6,

time: 17.8 us -> 17.6 us (0.989)
    pallas_call x1, Pallas kernels: 1.48 us -> 1.2 us  [shards(): pl.pallas_call(finish_kernel, name='finish', out_shape=results, in_specs=...]
  transfers between devices with their start and end apart: 5 -> 5, of which waited for: 3 -> 3; matrix products, arithmetic and copies ran while one was open for 0% -> 0% of each run, Pallas kernels for 6% -> 7%
where the time goes in v2:
time: 17.6 us; the launch traced here: 17.4 us
  starting transfers between devices  8.31 us (47%)
  waiting for transfers between devices  4.5 us (26%)
  Pallas kernels  3.9 us (22%)
  between operations  0.67 us (4%)
    ppermute x5, starting transfers between devices, gather_blocks(): pieces.append(lax.ppermute(held, 'visits', partner))  8.31 us
    ppermute x5, waiting for transfers between devices, gather_blocks(): pieces.append(lax.ppermute(held, 'visits', partner))  4.5 us
    pallas_call x1, Pallas kernels, shards(): pl.pallas_call(match_kernel, name='match', out_shape=(pltpu.VMEM(exposure...  1.47 us
    pallas_call x1, Pallas kernels, shards(): pl.pallas_call(finish_kernel, name='finish', out_shape=results, in_specs=...  1.2 us
    pallas_call x1, Pallas kernels, shards(): pl.pallas_call(prep_kernel, name='prep', out_shape=tuple((pltpu.VMEM(shap...  1.01 us
  transfers between devices with their start and end apart: 5, of which 3 were waited for; matrix products, arithmetic and copies ran while one was open for 0% of the time, Pallas kernels for 7%

profile of v2, /device:TPU:0, one launch (start us, length us, event | category | flops | bytes accessed | tf_op | source)
XLA Modules:
  0.0 17.4 jit_solution(16066911368045581580)
XLA Ops:
  0.6 1.5 %match.1 = (f32[7,8,128]{2,1,0:T(8,128)S(1)}, bf16[64,128]{1,0:T(8,128)(2,1)S(1)}) custom-call(f32[7,8,128]{2,1,0:T(8,128)} %refs_0_.1, s32[6,7]{1,0:T(8,128)} %refs_1_.1, f32[2,4,21]{2,1,0:T(4,128)} %psf_basis.1, f32[2,4,7]{2,1,0:T(4,128)} %psf_weights.1, s32[7]{0:T(128)} %patch_of.1), custom_call_target="tpu_custom_call" | custom-call | tf_op jit(solution)/shard_map/match/pallas_call | solution.py:416
  2.1 4.6 %collective-permute-start = (bf16[64,128]{1,0:T(8,128)(2,1)S(1)}, bf16[64,128]{1,0:T(8,128)(2,1)S(1)}, u32[]{:S(2)}, u32[]{:S(2)}) collective-permute-start(bf16[64,128]{1,0:T(8,128)(2,1)S(1)} %get-tuple-element.13), channel_id=1, source_target_pairs={{0,13},{1,12},{2,15},{3,14},{4,9},{5,8},{6,11},{7,10},{8,5},{9,4},... | collective-permute-start | bytes 49160 | tf_op jit(solution)/shard_map/ppermute | solution.py:384
  6.7 1.5 %collective-permute-done = bf16[64,128]{1,0:T(8,128)(2,1)S(1)} collective-permute-done((bf16[64,128]{1,0:T(8,128)(2,1)S(1)}, bf16[64,128]{1,0:T(8,128)(2,1)S(1)}, u32[]{:S(2)}, u32[]{:S(2)}) %collective-permute-start) | collective-permute-done | bytes 16416 | tf_op jit(solution)/shard_map/ppermute | solution.py:384
  8.2 1.0 %collective-permute-start.1 = (bf16[128,128]{1,0:T(8,128)(2,1)S(1)}, bf16[128,128]{1,0:T(8,128)(2,1)S(1)}, u32[]{:S(2)}, u32[]{:S(2)}) collective-permute-start(bf16[128,128]{1,0:T(8,128)(2,1)S(1)} %get-tuple-element.23), channel_id=1, source_target_pairs={{0,7},{1,6},{2,5},{3,4},{4,3},{5,2},{6,1},{7,0},{8,15},{9,14},{10,... | collective-permute-start | bytes 98312 | tf_op jit(solution)/shard_map/ppermute | solution.py:384
  9.2 2.2 %collective-permute-start.3 = (bf16[128,128]{1,0:T(8,128)(2,1)S(1)}, bf16[128,128]{1,0:T(8,128)(2,1)S(1)}, u32[]{:S(2)}, u32[]{:S(2)}) collective-permute-start(bf16[128,128]{1,0:T(8,128)(2,1)S(1)} %get-tuple-element.23), channel_id=1, source_target_pairs={{0,5},{1,4},{2,7},{3,6},{4,1},{5,0},{6,3},{7,2},{8,13},{9,12},{10,... | collective-permute-start | bytes 98312 | tf_op jit(solution)/shard_map/ppermute | solution.py:384
  11.4 0.3 %collective-permute-start.2 = (bf16[128,128]{1,0:T(8,128)(2,1)S(1)}, bf16[128,128]{1,0:T(8,128)(2,1)S(1)}, u32[]{:S(2)}, u32[]{:S(2)}) collective-permute-start(bf16[128,128]{1,0:T(8,128)(2,1)S(1)} %get-tuple-element.23), channel_id=1, source_target_pairs={{0,3},{1,2},{2,1},{3,0},{4,7},{5,6},{6,5},{7,4},{8,11},{9,10},{10,... | collective-permute-start | bytes 98312 | tf_op jit(solution)/shard_map/ppermute | solution.py:384
  11.7 0.8 %collective-permute-done.1 = bf16[128,128]{1,0:T(8,128)(2,1)S(1)} collective-permute-done((bf16[128,128]{1,0:T(8,128)(2,1)S(1)}, bf16[128,128]{1,0:T(8,128)(2,1)S(1)}, u32[]{:S(2)}, u32[]{:S(2)}) %collective-permute-start.1) | collective-permute-done | bytes 32800 | tf_op jit(solution)/shard_map/ppermute | solution.py:384
  12.5 2.2 %collective-permute-done.2 = bf16[128,128]{1,0:T(8,128)(2,1)S(1)} collective-permute-done((bf16[128,128]{1,0:T(8,128)(2,1)S(1)}, bf16[128,128]{1,0:T(8,128)(2,1)S(1)}, u32[]{:S(2)}, u32[]{:S(2)}) %collective-permute-start.2) | collective-permute-done | bytes 32800 | tf_op jit(solution)/shard_map/ppermute | solution.py:384
  14.7 0.0 collective-permute-done.3
  14.7 0.2 %collective-permute-start.4 = (bf16[512,128]{1,0:T(8,128)(2,1)S(1)}, bf16[512,128]{1,0:T(8,128)(2,1)S(1)}, u32[]{:S(2)}, u32[]{:S(2)}) collective-permute-start(bf16[512,128]{1,0:T(8,128)(2,1)S(1)} %constant_dynamic-update-slice_fusion.2.block), channel_id=1, source_target_pairs={{0,1},{1,0},{2,3},{3,2},{4,5},{5,4},{6,7},{7,6},{8,9},{9,8},{10,11... | collective-permute-start | bytes 393224 | tf_op jit(solution)/shard_map/ppermute | solution.py:384
  15.0 1.0 %prep.1 = (f32[8,8,128]{2,1,0:T(8,128)S(1)}, bf16[256,512]{1,0:T(8,128)(2,1)S(1)}, f32[4,21,8,128]{3,2,1,0:T(8,128)S(1)}, f32[4,7,8,128]{3,2,1,0:T(8,128)S(1)}, ...) custom-call(s32[7]{0:T(128)} %patch_of.1, f32[2,4,7]{2,1,0:T(4,128)} %psf_weights.1, f32[2,4,21]{2,1,0:T(4,128)} %psf_basis.1, ...), custom_call_target="tpu_custom_call" | custom-call | tf_op jit(solution)/shard_map/prep/pallas_call | solution.py:453
  16.0 0.2 %sift.1 = (f32[8,8,8,128]{3,2,1,0:T(8,128)S(1)}, f32[8,8,128]{2,1,0:T(8,128)S(1)}) custom-call(bf16[512,128]{1,0:T(8,128)(2,1)S(1)} %constant_dynamic-update-slice_fusion.2.block, f32[8,8,128]{2,1,0:T(8,128)S(1)} %get-tuple-element.15.goals), custom_call_target="tpu_custom_call" | custom-call | tf_op jit(solution)/shard_map/sift/pallas_call | solution.py:471
  16.2 0.0 collective-permute-done.4.block
  16.2 1.2 %finish.1 = (bf16[1,8,128]{2,1,0:T(8,128)(2,1)}, f32[7,8,128]{2,1,0:T(8,128)}, f32[7,8,128]{2,1,0:T(8,128)}) custom-call(bf16[512,128]{1,0:T(8,128)(2,1)S(1)} %collective-permute-done.4.block, f32[7,8,128]{2,1,0:T(8,128)S(1)} %get-tuple-element.14.warped, f32[8,8,8,128]{3,2,1,0:T(8,128)S(1)} %get-tuple-element.16.ranked, ...), custom_call_target="tpu_custom_call" | custom-call | tf_op jit(solution)/shard_map/finish/pallas_call | solution.py:478
  (5 shorter events, 0.0 us)
Async XLA Ops:
  2.1 6.1 %collective-permute-start = (bf16[64,128]{1,0:T(8,128)(2,1)S(1)}, bf16[64,128]{1,0:T(8,128)(2,1)S(1)}, u32[]{:S(2)}, u32[]{:S(2)}) collective-permute-start(bf16[64,128]{1,0:T(8,128)(2,1)S(1)} %get-tuple-element.13), channel_id=1, source_target_pairs={{0,13},{1,12},{2,15},{3,14},{4,9},{5,8},{6,11},{7,10},{8,5},{9,4},... | collective-permute-start | bytes 49160 | tf_op jit(solution)/shard_map/ppermute | solution.py:384
  8.2 4.3 %collective-permute-start.1 = (bf16[128,128]{1,0:T(8,128)(2,1)S(1)}, bf16[128,128]{1,0:T(8,128)(2,1)S(1)}, u32[]{:S(2)}, u32[]{:S(2)}) collective-permute-start(bf16[128,128]{1,0:T(8,128)(2,1)S(1)} %get-tuple-element.23), channel_id=1, source_target_pairs={{0,7},{1,6},{2,5},{3,4},{4,3},{5,2},{6,1},{7,0},{8,15},{9,14},{10,... | collective-permute-start | bytes 98312 | tf_op jit(solution)/shard_map/ppermute | solution.py:384
  9.2 5.6 %collective-permute-start.3 = (bf16[128,128]{1,0:T(8,128)(2,1)S(1)}, bf16[128,128]{1,0:T(8,128)(2,1)S(1)}, u32[]{:S(2)}, u32[]{:S(2)}) collective-permute-start(bf16[128,128]{1,0:T(8,128)(2,1)S(1)} %get-tuple-element.23), channel_id=1, source_target_pairs={{0,5},{1,4},{2,7},{3,6},{4,1},{5,0},{6,3},{7,2},{8,13},{9,12},{10,... | collective-permute-start | bytes 98312 | tf_op jit(solution)/shard_map/ppermute | solution.py:384
  11.4 3.3 %collective-permute-start.2 = (bf16[128,128]{1,0:T(8,128)(2,1)S(1)}, bf16[128,128]{1,0:T(8,128)(2,1)S(1)}, u32[]{:S(2)}, u32[]{:S(2)}) collective-permute-start(bf16[128,128]{1,0:T(8,128)(2,1)S(1)} %get-tuple-element.23), channel_id=1, source_target_pairs={{0,3},{1,2},{2,1},{3,0},{4,7},{5,6},{6,5},{7,4},{8,11},{9,10},{10,... | collective-permute-start | bytes 98312 | tf_op jit(solution)/shard_map/ppermute | solution.py:384
  14.7 1.5 %collective-permute-start.4 = (bf16[512,128]{1,0:T(8,128)(2,1)S(1)}, bf16[512,128]{1,0:T(8,128)(2,1)S(1)}, u32[]{:S(2)}, u32[]{:S(2)}) collective-permute-start(bf16[512,128]{1,0:T(8,128)(2,1)S(1)} %constant_dynamic-update-slice_fusion.2.block), channel_id=1, source_target_pairs={{0,1},{1,0},{2,3},{3,2},{4,5},{5,4},{6,7},{7,6},{8,9},{9,8},{10,11... | collective-permute-start | bytes 393224 | tf_op jit(solution)/shard_map/ppermute | solution.py:384
